TPU v7x, 512 devices: a whole 4x8x8 slice. The times are simulated.
512 devices in a mesh: pipe: 8 (over z), ctx: 32 (over x, y_hi, core), tp: 2 (over y_lo).
Axes of the slice: x: 4, y: 8 (y_hi: 4, y_lo: 2; y = y_hi * 2 + y_lo), z: 8, core: 2. Of those that a mesh axis runs over, the one named last changes fastest.
Arguments:
- queries: bfloat16 [8, 2048, 128, 128], P('pipe', 'ctx', 'tp'), may hold values from -10 to 10
- span_keys: bfloat16 [8, 2048, 8, 128], P('pipe', 'ctx', 'tp'), may hold values from -6 to 6
- span_values: bfloat16 [8, 2048, 8, 128], P('pipe', 'ctx', 'tp'), may hold values from -12 to 12
- cache_keys: bfloat16 [8, 1024, 8, 128], P('pipe', 'ctx', 'tp'), may hold values from -6 to 6
- cache_values: bfloat16 [8, 1024, 8, 128], P('pipe', 'ctx', 'tp'), may hold values from -6 to 6
- scale_exps: int32 [8, 64, 8, 2], P('pipe', 'ctx', 'tp'), may hold values from -3 to 1
- block_order: int32 [8, 64], P('pipe'), may hold values from 0 to 63, each once within a row
Outputs:
- handed: bfloat16 [8, 2048, 128, 128], P('pipe', 'ctx', 'tp')
All inputs are finite; a program needn't handle non-finite values.
Results may differ from a plain program's by a relative error of at most 0.006.
Values may be sent and summed in bfloat16 or wider, within the bound.
No kernel may reach another device: no remote copies, remote signals or barrier semaphores. Data moves between devices by JAX's collectives and lax.ppermute only.
A program may use at most 128 MiB of HBM per device.

v0:
```python
import functools
import math

import jax
import jax.numpy as jnp
from jax import lax
from jax.experimental import pallas as pl
from jax.experimental.pallas import tpu as pltpu
from jax.sharding import Mesh, PartitionSpec as P


CBLK = 16
HALF = 32
HD = 128
GROUP = 16
FAR = -(2.0**100)
FLAT = ("pipe", "x", "y", "core")


def moved(value, sizes, dz=0, dx=0, dc=0):
    nz, nx, ny, nc = sizes
    pairs = []
    for z in range(nz):
        for x in range(nx):
            for y in range(ny):
                for c in range(nc):
                    source = ((z * nx + x) * ny + y) * nc + c
                    target = ((((z + dz) % nz) * nx + (x + dx) % nx) * ny + y) * nc + (c ^ dc)
                    pairs.append((source, target))
    return lax.ppermute(value, FLAT, pairs)


def iota(shape, axis):
    return lax.broadcasted_iota(jnp.int32, shape, axis)


def pick(rows, width, first, per_head, heads, scale=None):
    out = iota((rows, width), 0)
    src = iota((rows, width), 1)
    head = first + out // per_head
    token = out % per_head
    hit = src == token * heads + head
    if scale is None:
        return jnp.where(hit, 1.0, 0.0).astype(jnp.bfloat16)
    return jnp.where(hit, scale(token // CBLK, head), 0.0).astype(jnp.bfloat16)


def hadamard_signs():
    bits = iota((HD, HD), 0) & iota((HD, HD), 1)
    bits = bits ^ (bits >> 4)
    bits = bits ^ (bits >> 2)
    bits = (bits ^ (bits >> 1)) & 1
    return (1.0 - 2.0 * bits.astype(jnp.float32)).astype(jnp.bfloat16)


def pack_body(core_ref, exps_ref, order_ref, sk_ref, sv_ref, ck_ref, cv_ref, own_ref, other_ref, *, heads):
    core = core_ref[0]
    tok = sk_ref.shape[0] // heads
    cache = ck_ref.shape[0] // heads
    signs = hadamard_signs()
    for which, ref in ((0, own_ref), (1, other_ref)):
        first = 2 * (core if which == 0 else 1 - core)
        span_pick = pick(2 * tok, heads * tok, first, tok, heads)
        for kv, (span, cached) in enumerate(((sk_ref, ck_ref), (sv_ref, cv_ref))):

            def scale(block, head):
                value = jnp.ones(block.shape, jnp.float32)
                for b in range(cache // CBLK):
                    for h in range(heads):
                        power = (jnp.int32(1) << (exps_ref[b, kv, h] + 3)).astype(jnp.float32) * 0.125
                        value = jnp.where((block == b) & (head == h), power, value)
                return value

            cache_pick = pick(2 * cache, heads * cache, first, cache, heads, scale)
            moved_span = jnp.dot(span_pick, span[...], preferred_element_type=jnp.float32).astype(jnp.bfloat16)
            moved_cache = jnp.dot(cache_pick, cached[...], preferred_element_type=jnp.float32).astype(jnp.bfloat16)
            if kv == 1:
                moved_span = jnp.dot(moved_span, signs, preferred_element_type=jnp.float32).astype(jnp.bfloat16)
                moved_cache = jnp.dot(moved_cache, signs, preferred_element_type=jnp.float32).astype(jnp.bfloat16)
            for h in range(2):
                at = (2 * h + kv) * (cache + tok)
                ref[at : at + cache] = moved_cache[h * cache : (h + 1) * cache]
                ref[at + cache : at + cache + tok] = moved_span[h * tok : (h + 1) * tok]
    order = order_ref[...].astype(jnp.float32)
    order = jnp.concatenate([order, jnp.zeros((1, HD - order.shape[1]), jnp.float32)], axis=1)
    own_ref[4 * (cache + tok) :] = jnp.broadcast_to(order, (16, HD)).astype(jnp.bfloat16)


def pack(core, exps, order, span_keys, span_values, cache_keys, cache_values):
    tok, heads, width = span_keys.shape
    cache = cache_keys.shape[0]
    flat = lambda a: a.reshape(-1, width)
    rows = 4 * (cache + tok)
    smem = pl.BlockSpec(memory_space=pltpu.SMEM)
    vmem = pl.BlockSpec(memory_space=pltpu.VMEM)
    return pl.pallas_call(
        functools.partial(pack_body, heads=heads),
        out_shape=(jax.ShapeDtypeStruct((rows + 16, width), jnp.bfloat16), jax.ShapeDtypeStruct((rows, width), jnp.bfloat16)),
        in_specs=[smem, smem, vmem, vmem, vmem, vmem, vmem],
        out_specs=(vmem, vmem),
        name="pack_kv",
    )(core, exps, order, flat(span_keys), flat(span_values), flat(cache_keys), flat(cache_values))


def fill(place_ref, order_ref, chunk_refs, spots, ka, va, head_slot, tok, cache):
    x, y, core = place_ref[0], place_ref[1], place_ref[2]
    nx, ny = place_ref[3], place_ref[4]
    halves = tok // HALF
    lane = iota((HALF, HD), 1)
    within = iota((HALF, HD), 0)
    slot = lane // HALF
    base = jnp.zeros((HALF, HD), jnp.int32)
    for s in range(2 * halves):
        owner = (x * ny + y) * 2 + (core if s < halves else 1 - core)
        base = jnp.where(slot == s, order_ref[0, owner * halves + s % halves], base)
    pos_query = base * HALF + lane % HALF
    rows = cache + tok
    places = []
    for ref, (shift, first_y) in zip(chunk_refs, spots):
        for k in range(ref.shape[0]):
            for cc in range(2):
                owner = ((x + shift) % nx * ny + first_y + k) * 2 + (core if cc == 0 else 1 - core)
                places.append((ref, k, cc, owner))

    @pl.when(head_slot == 0)
    def _():
        for n, (_, _, _, owner) in enumerate(places):
            at = n * rows
            ka[at : at + cache, HD:] = jnp.zeros((cache, HD), jnp.bfloat16)
            for b in range(halves):
                pos_key = order_ref[0, owner * halves + b] * HALF + within
                start = at + cache + b * HALF
                ka[start : start + HALF, HD:] = jnp.where(pos_key <= pos_query, 0.0, FAR).astype(jnp.bfloat16)
        va[:, HD:] = jnp.ones((va.shape[0], HD), jnp.bfloat16)

    for n, (ref, k, cc, _) in enumerate(places):
        at = n * rows
        ka[at : at + rows, :HD] = ref[k, cc, head_slot, 0]
        va[at : at + rows, :HD] = ref[k, cc, head_slot, 1]


def stage_body(*refs, nchunk, spots, first, last, tok, cache, sub, ahead):
    place_ref, order_ref = refs[0], refs[1]
    refs = refs[2:]
    q_refs, refs = refs[:2], refs[2:]
    chunk_refs, refs = refs[:nchunk], refs[nchunk:]
    if not first:
        (acc_in, max_in), refs = refs[:2], refs[2:]
    if last:
        (own_ref, other_ref), refs = refs[:2], refs[2:]
    else:
        (acc_out, max_out), refs = refs[:2], refs[2:]
    ka, va = refs
    fill(place_ref, order_ref, chunk_refs, spots, ka, va, pl.program_id(0), tok, cache)
    factor = math.log2(math.e) / math.sqrt(HD)
    toks = sub // GROUP
    pieces = 2 * tok // toks

    def scores(s):
        tok0 = s * toks
        ref = q_refs[tok0 // tok]
        part = ref[tok0 % tok : tok0 % tok + toks].reshape(sub, HD)
        token = tok0 + iota((sub, HD), 0) // GROUP
        hot = jnp.where(iota((sub, HD), 1) == token, 1.0, 0.0).astype(jnp.bfloat16)
        left = jnp.concatenate([part, hot], axis=1)
        return lax.dot_general(left, ka[...], (((1,), (1,)), ((), ())), preferred_element_type=jnp.float32)

    ready = [scores(s) for s in range(ahead)]
    for s in range(pieces):
        if s + ahead < pieces:
            ready.append(scores(s + ahead))
        score = ready[s]
        ready[s] = None
        span = slice(s * sub, (s + 1) * sub)
        top = jnp.max(score, axis=1, keepdims=True)
        if not first:
            top_old = max_in[0, span, :1]
            top = jnp.maximum(top, top_old)
        weight = jnp.exp2((score - top) * factor).astype(jnp.bfloat16)
        acc = jnp.dot(weight, va[...], preferred_element_type=jnp.float32)
        if not first:
            acc = acc + acc_in[0, span] * jnp.exp2((top_old - top) * factor)
        if last:
            mixed = acc[:, :HD] * (1.0 / (acc[:, HD:] * math.sqrt(HD)))
            ref = (own_ref, other_ref)[s * toks // tok]
            ref[s * toks % tok : s * toks % tok + toks] = mixed.astype(jnp.bfloat16).reshape(toks, GROUP, HD)
        else:
            acc_out[0, span] = acc
            max_out[0, span] = jnp.broadcast_to(top, (sub, HD))


def stage(place, order, queries, chunks, spots, state, tok, cache, last=False, sub=512, ahead=1):
    total = 2 * tok * GROUP
    keys = sum(c.shape[0] for c in chunks) * 2 * (cache + tok)
    first = state is None
    in_specs = [pl.BlockSpec(memory_space=pltpu.SMEM)]
    for _ in queries:
        in_specs.append(pl.BlockSpec((tok, GROUP, HD), lambda h, p: (0, 2 * p[2] + h, 0)))
    for c in chunks:
        in_specs.append(pl.BlockSpec(c.shape, lambda h, p, nd=c.ndim: (0,) * nd, pipeline_mode=pl.Buffered(1)))
    acc_spec = pl.BlockSpec((1, total, 2 * HD), lambda h, p: (h, 0, 0))
    max_spec = pl.BlockSpec((1, total, HD), lambda h, p: (h, 0, 0))
    operands = [order, *queries, *chunks]
    if not first:
        in_specs += [acc_spec, max_spec]
        operands += list(state)
    if last:
        out_specs = (
            pl.BlockSpec((tok, GROUP, HD), lambda h, p: (0, 2 * p[2] + h, 0)),
            pl.BlockSpec((tok, GROUP, HD), lambda h, p: (0, h, 0)),
        )
        out_shape = (
            jax.ShapeDtypeStruct((tok, 4 * GROUP, HD), jnp.bfloat16),
            jax.ShapeDtypeStruct((tok, 2 * GROUP, HD), jnp.bfloat16),
        )
    else:
        out_specs = (acc_spec, max_spec)
        out_shape = (
            jax.ShapeDtypeStruct((2, total, 2 * HD), jnp.float32),
            jax.ShapeDtypeStruct((2, total, HD), jnp.float32),
        )
    body = functools.partial(
        stage_body, nchunk=len(chunks), spots=spots, first=first, last=last, tok=tok, cache=cache, sub=sub, ahead=ahead
    )
    return pl.pallas_call(
        body,
        grid_spec=pltpu.PrefetchScalarGridSpec(
            num_scalar_prefetch=1,
            grid=(2,),
            in_specs=in_specs,
            out_specs=out_specs,
            scratch_shapes=[pltpu.VMEM((keys, 2 * HD), jnp.bfloat16), pltpu.VMEM((keys, 2 * HD), jnp.bfloat16)],
        ),
        out_shape=out_shape,
        compiler_params=pltpu.CompilerParams(vmem_limit_bytes=24 << 20),
        cost_estimate=pl.CostEstimate(flops=2 * 2 * total * keys * 4 * HD, transcendentals=2 * total * keys, bytes_accessed=12 << 20),
        name="stage_last" if last else "stage",
    )(place, *operands)


def put_body(place_ref, part_ref, whole_ref, out_ref, sems):
    tok, heads = part_ref.shape[:2]
    count = sems.shape[0]
    step = tok // count
    copies = []
    for n in range(count):
        span = pl.ds(n * step, step)
        target = out_ref.at[span, pl.ds((1 - place_ref[2]) * heads, heads)]
        copies.append(pltpu.make_async_copy(part_ref.at[span], target, sems.at[n]))
    for copy in copies:
        copy.start()
    for copy in copies:
        copy.wait()


def put(place, part, whole):
    raw = pl.BlockSpec(memory_space=pl.ANY)
    return pl.pallas_call(
        put_body,
        out_shape=jax.ShapeDtypeStruct(whole.shape, whole.dtype),
        in_specs=[pl.BlockSpec(memory_space=pltpu.SMEM), raw, raw],
        out_specs=raw,
        scratch_shapes=[pltpu.SemaphoreType.DMA((4,))],
        input_output_aliases={2: 0},
        compiler_params=pltpu.CompilerParams(vmem_limit_bytes=1 << 20),
        name="put",
    )(place, part, whole)


def on_device(queries, span_keys, span_values, cache_keys, cache_values, scale_exps, block_order, sizes):
    return relay(queries, span_keys, span_values, cache_keys, cache_values, scale_exps, block_order, sizes)


def relay(queries, span_keys, span_values, cache_keys, cache_values, scale_exps, block_order, sizes):
    _, nx, ny, nc = sizes
    tok, _, width = queries.shape[1:]
    cache = cache_keys.shape[1]
    core = lax.axis_index("core").astype(jnp.int32)
    place = jnp.stack([lax.axis_index("x").astype(jnp.int32), lax.axis_index("y").astype(jnp.int32), core, jnp.int32(nx), jnp.int32(ny)])
    exps = scale_exps[0].transpose(0, 2, 1)
    own, other = pack(core.reshape(1), exps, block_order, span_keys[0], span_values[0], cache_keys[0], cache_values[0])
    own = moved(own, sizes, dz=1)
    other = moved(other, sizes, dz=1, dc=1)
    rows = 4 * (cache + tok)
    order = own[rows : rows + 1, : block_order.shape[1]].astype(jnp.int32)
    q_own = moved(queries[0], sizes, dz=1)
    q_other = moved(q_own, sizes, dc=1)
    mine = jnp.concatenate([own[:rows], other], axis=0)
    line = lax.all_gather(mine, "y", axis=0, tiled=True)
    parts = lambda a: a.reshape(-1, nc, 2, 2, cache + tok, width)
    half = line.shape[0] // 2
    low, high = line[:half], line[half:]
    near_a = moved(low, sizes, dx=1)
    near_b = moved(high, sizes, dx=-1)
    rest_a = moved(high, sizes, dx=1)
    rest_b = moved(low, sizes, dx=-1)
    far_a = moved(near_a, sizes, dx=1)
    far_b = moved(near_b, sizes, dx=-1)
    mid = ny // 2
    spots = [(0, 0), (nx - 1, 0), (1, mid)]
    state = stage(place, order, [q_own, q_other], [parts(line), parts(near_a), parts(near_b)], spots, None, tok, cache)
    chunks = [parts(rest_a), parts(rest_b), parts(far_a), parts(far_b)]
    spots = [(nx - 1, mid), (1, 0), (2, 0), (2, mid)]
    result, theirs = stage(place, order, [q_own, q_other], chunks, spots, state, tok, cache, last=True, ahead=3)
    theirs = moved(theirs, sizes, dc=1)
    return put(place, theirs, result)[None]


def solution(mesh):
    nz, nctx, ntp = mesh.devices.shape
    nx = ny = 4
    nc = nctx // (nx * ny)
    fine = Mesh(mesh.devices.reshape(nz, nx, ny, nc, ntp), ("pipe", "x", "y", "core", "tp"))
    split = P("pipe", ("x", "y", "core"), "tp", None)
    return jax.shard_map(
        functools.partial(on_device, sizes=(nz, nx, ny, nc)),
        mesh=fine,
        in_specs=(split,) * 6 + (P("pipe", None),),
        out_specs=split,
        check_vma=False,
    )
```

profile of v0, /device:TPU:1, one launch (start us, length us, event | category | flops | bytes accessed | tf_op | source)
XLA Modules:
  0.0 112.9 jit_solution(3770395757510537088)
XLA Ops:
  0.0 4.8 %collective-permute-start.1 = (bf16[64,64,128]{2,1,0:T(8,128)(2,1)}, bf16[64,64,128]{2,1,0:T(8,128)(2,1)S(1)}, u32[]{:S(2)}, u32[]{:S(2)}) collective-permute-start(bf16[64,64,128]{2,1,0:T(8,128)(2,1)} %bitcast.30), channel_id=1, source_target_pairs={{0,64},{2,66},{4,68},{6,70},{8,72},{10,74},{12,76},{14,78},{16,80}... | collective-permute-start | bytes 3145736 | tf_op jit(solution)/shard_map/ppermute | solution.py:30
  4.8 2.1 %pack_kv.1 = (bf16[400,128]{1,0:T(8,128)(2,1)}, bf16[384,128]{1,0:T(8,128)(2,1)}) custom-call(s32[1]{0:T(128)} %bitcast.2.core_ref, s32[2,2,4]{2,1,0:T(2,128)} %bitcast.29, s32[1,64]{1,0:T(1,128)} %order_ref.1, bf16[256,128]{1,0:T(8,128)(2,1)} %bitcast.25, bf16[256,128]{1,0:T(8,128)(2,1)} %bitcast.26, bf16[128,128]{1,0:T(8,128)(2,1)} %bitcast.27, ...), custom_call_target="tpu_custom_call" | custom-call | tf_op jit(solution)/shard_map/pack_kv/pallas_call | solution.py:96
  6.9 4.0 %collective-permute-start = (bf16[400,128]{1,0:T(8,128)(2,1)}, bf16[400,128]{1,0:T(8,128)(2,1)S(1)}, u32[]{:S(2)}, u32[]{:S(2)}) collective-permute-start(bf16[400,128]{1,0:T(8,128)(2,1)} %get-tuple-element.11), channel_id=1, source_target_pairs={{0,64},{2,66},{4,68},{6,70},{8,72},{10,74},{12,76},{14,78},{16,80}... | collective-permute-start | bytes 307208 | tf_op jit(solution)/shard_map/ppermute | solution.py:30
  10.9 5.1 %collective-permute-start.3 = (bf16[384,128]{1,0:T(8,128)(2,1)}, bf16[384,128]{1,0:T(8,128)(2,1)S(1)}, u32[]{:S(2)}, u32[]{:S(2)}) collective-permute-start(bf16[384,128]{1,0:T(8,128)(2,1)} %get-tuple-element.12), channel_id=1, source_target_pairs={{0,66},{2,64},{4,70},{6,68},{8,74},{10,72},{12,78},{14,76},{16,82}... | collective-permute-start | bytes 294920 | tf_op jit(solution)/shard_map/ppermute | solution.py:30
  16.0 20.7 %collective-permute-done = bf16[400,128]{1,0:T(8,128)(2,1)S(1)} collective-permute-done((bf16[400,128]{1,0:T(8,128)(2,1)}, bf16[400,128]{1,0:T(8,128)(2,1)S(1)}, u32[]{:S(2)}, u32[]{:S(2)}) %collective-permute-start) | collective-permute-done | bytes 102432 | tf_op jit(solution)/shard_map/ppermute | solution.py:30
  36.7 2.7 %collective-permute-done.3 = bf16[384,128]{1,0:T(8,128)(2,1)S(1)} collective-permute-done((bf16[384,128]{1,0:T(8,128)(2,1)}, bf16[384,128]{1,0:T(8,128)(2,1)S(1)}, u32[]{:S(2)}, u32[]{:S(2)}) %collective-permute-start.3) | collective-permute-done | bytes 98336 | tf_op jit(solution)/shard_map/ppermute | solution.py:30
  39.4 0.0 collective-permute-done.1.refs_2_
  39.4 1.9 %collective-permute-start.2 = (bf16[64,64,128]{2,1,0:T(8,128)(2,1)S(1)}, bf16[64,64,128]{2,1,0:T(8,128)(2,1)S(1)}, u32[]{:S(2)}, u32[]{:S(2)}) collective-permute-start(bf16[64,64,128]{2,1,0:T(8,128)(2,1)S(1)} %collective-permute-done.1.refs_2_), channel_id=1, source_target_pairs={{0,2},{2,0},{4,6},{6,4},{8,10},{10,8},{12,14},{14,12},{16,18},{18,... | collective-permute-start | bytes 3145736 | tf_op jit(solution)/shard_map/ppermute | solution.py:30
  41.4 18.3 %all_gather.3 = bf16[3072,128]{1,0:T(8,128)(2,1)S(1)} all-gather(bf16[768,128]{1,0:T(8,128)(2,1)S(1)} %pad_maximum_fusion), channel_id=1, replica_groups=mesh['pipe'=8,'x'=4,'y'=4,'core'=2,'tp'=2] {'y'}, dimensions={0}, use_global_device_ids=true | all-gather | bytes 983040 | tf_op jit(solution)/shard_map/all_gather | solution.py:289
  59.6 0.9 fusion
  60.6 3.1 %collective-permute-start.6 = (bf16[1536,128]{1,0:T(8,128)(2,1)}, bf16[1536,128]{1,0:T(8,128)(2,1)S(1)}, u32[]{:S(2)}, u32[]{:S(2)}) collective-permute-start(bf16[1536,128]{1,0:T(8,128)(2,1)} %get-tuple-element.17), channel_id=1, source_target_pairs={{0,16},{2,18},{4,20},{6,22},{8,24},{10,26},{12,28},{14,30},{16,32}... | collective-permute-start | bytes 1179656 | tf_op jit(solution)/shard_map/ppermute | solution.py:30
  63.7 3.4 %collective-permute-start.8 = (bf16[1536,128]{1,0:T(8,128)(2,1)}, bf16[1536,128]{1,0:T(8,128)(2,1)}, u32[]{:S(2)}, u32[]{:S(2)}) collective-permute-start(bf16[1536,128]{1,0:T(8,128)(2,1)} %get-tuple-element.18), channel_id=1, source_target_pairs={{0,48},{2,50},{4,52},{6,54},{8,56},{10,58},{12,60},{14,62},{16,0},... | collective-permute-start | bytes 1179656 | tf_op jit(solution)/shard_map/ppermute | solution.py:30
  67.1 0.1 pad_add_fusion.refs_0_.place_ref
  67.2 3.2 %collective-permute-start.5 = (bf16[1536,128]{1,0:T(8,128)(2,1)}, bf16[1536,128]{1,0:T(8,128)(2,1)S(1)}, u32[]{:S(2)}, u32[]{:S(2)}) collective-permute-start(bf16[1536,128]{1,0:T(8,128)(2,1)} %get-tuple-element.17), channel_id=1, source_target_pairs={{0,48},{2,50},{4,52},{6,54},{8,56},{10,58},{12,60},{14,62},{16,0},... | collective-permute-start | bytes 1179656 | tf_op jit(solution)/shard_map/ppermute | solution.py:30
  70.3 2.1 %collective-permute-start.4 = (bf16[1536,128]{1,0:T(8,128)(2,1)}, bf16[1536,128]{1,0:T(8,128)(2,1)S(1)}, u32[]{:S(2)}, u32[]{:S(2)}) collective-permute-start(bf16[1536,128]{1,0:T(8,128)(2,1)} %get-tuple-element.18), channel_id=1, source_target_pairs={{0,16},{2,18},{4,20},{6,22},{8,24},{10,26},{12,28},{14,30},{16,32}... | collective-permute-start | bytes 1179656 | tf_op jit(solution)/shard_map/ppermute | solution.py:30
  72.5 0.0 collective-permute-done.6
  72.5 1.9 %collective-permute-start.7 = (bf16[1536,128]{1,0:T(8,128)(2,1)S(1)}, bf16[1536,128]{1,0:T(8,128)(2,1)S(1)}, u32[]{:S(2)}, u32[]{:S(2)}) collective-permute-start(bf16[1536,128]{1,0:T(8,128)(2,1)S(1)} %collective-permute-done.6), channel_id=1, source_target_pairs={{0,16},{2,18},{4,20},{6,22},{8,24},{10,26},{12,28},{14,30},{16,32}... | collective-permute-start | bytes 1179656 | tf_op jit(solution)/shard_map/ppermute | solution.py:30
  74.4 0.0 collective-permute-done.8
  74.4 4.6 %collective-permute-start.9 = (bf16[1536,128]{1,0:T(8,128)(2,1)}, bf16[1536,128]{1,0:T(8,128)(2,1)S(1)}, u32[]{:S(2)}, u32[]{:S(2)}) collective-permute-start(bf16[1536,128]{1,0:T(8,128)(2,1)} %collective-permute-done.8), channel_id=1, source_target_pairs={{0,48},{2,50},{4,52},{6,54},{8,56},{10,58},{12,60},{14,62},{16,0},... | collective-permute-start | bytes 1179656 | tf_op jit(solution)/shard_map/ppermute | solution.py:30
  79.0 0.0 collective-permute-done.2.refs_3_
  79.0 10.4 %stage.1 = (f32[2,2048,256]{2,1,0:T(8,128)S(1)}, f32[2,2048,128]{2,1,0:T(8,128)S(1)}) custom-call(s32[5]{0:T(128)S(1)} %pad_add_fusion.refs_0_.place_ref, s32[1,64]{1,0:T(1,128)S(1)} %slice_convert_fusion.refs_1_, bf16[64,64,128]{2,1,0:T(8,128)(2,1)S(1)} %collective-permute-done.1.refs_2_, bf16[64,64,128]{2,1,0:T(8,128)(2,1)S(1)} %collective-permute-done.2.refs_3_, ...), custom_call_target="tpu_custom_call" | custom-call | flops 6442450944 | bytes 12582912 | tf_op jit(solution)/shard_map/stage/pallas_call | solution.py:225
  89.4 0.0 collective-permute-done.5
  89.4 0.0 collective-permute-done.4
  89.4 0.0 collective-permute-done.7
  89.4 0.0 collective-permute-done.9
  89.4 10.5 %stage_last.1 = (bf16[64,64,128]{2,1,0:T(8,128)(2,1)}, bf16[64,32,128]{2,1,0:T(8,128)(2,1)S(1)}) custom-call(s32[5]{0:T(128)S(1)} %pad_add_fusion.refs_0_.place_ref, s32[1,64]{1,0:T(1,128)S(1)} %slice_convert_fusion.refs_1_, bf16[64,64,128]{2,1,0:T(8,128)(2,1)S(1)} %collective-permute-done.1.refs_2_, ...), custom_call_target="tpu_custom_call" | custom-call | flops 6442450944 | bytes 12582912 | tf_op jit(solution)/shard_map/stage_last/pallas_call | solution.py:225
  100.0 10.1 %collective-permute-start.10 = (bf16[64,32,128]{2,1,0:T(8,128)(2,1)S(1)}, bf16[64,32,128]{2,1,0:T(8,128)(2,1)S(1)}, u32[]{:S(2)}, u32[]{:S(2)}) collective-permute-start(bf16[64,32,128]{2,1,0:T(8,128)(2,1)S(1)} %get-tuple-element.15), channel_id=1, source_target_pairs={{0,2},{2,0},{4,6},{6,4},{8,10},{10,8},{12,14},{14,12},{16,18},{18,... | collective-permute-start | bytes 1572872 | tf_op jit(solution)/shard_map/ppermute | solution.py:30
  110.1 1.5 %collective-permute-done.10.part_ref = bf16[64,32,128]{2,1,0:T(8,128)(2,1)S(1)} collective-permute-done((bf16[64,32,128]{2,1,0:T(8,128)(2,1)S(1)}, bf16[64,32,128]{2,1,0:T(8,128)(2,1)S(1)}, u32[]{:S(2)}, u32[]{:S(2)}) %collective-permute-start.10) | collective-permute-done | bytes 524320 | tf_op jit(solution)/shard_map/ppermute | solution.py:30
  111.6 1.4 %put.1 = bf16[64,64,128]{2,1,0:T(8,128)(2,1)} custom-call(s32[5]{0:T(128)S(1)} %pad_add_fusion.refs_0_.place_ref, bf16[64,32,128]{2,1,0:T(8,128)(2,1)S(1)} %collective-permute-done.10.part_ref, bf16[64,64,128]{2,1,0:T(8,128)(2,1)} %get-tuple-element.16.whole_ref), custom_call_target="tpu_custom_call", output_to_operand_aliasing={{}: (2, {})} | custom-call | tf_op jit(solution)/shard_map/put/pallas_call | solution.py:258
  (4 shorter events, 0.0 us)
Async XLA Ops:
  0.0 39.4 %collective-permute-start.1 = (bf16[64,64,128]{2,1,0:T(8,128)(2,1)}, bf16[64,64,128]{2,1,0:T(8,128)(2,1)S(1)}, u32[]{:S(2)}, u32[]{:S(2)}) collective-permute-start(bf16[64,64,128]{2,1,0:T(8,128)(2,1)} %bitcast.30), channel_id=1, source_target_pairs={{0,64},{2,66},{4,68},{6,70},{8,72},{10,74},{12,76},{14,78},{16,80}... | collective-permute-start | bytes 3145736 | tf_op jit(solution)/shard_map/ppermute | solution.py:30
  6.9 29.9 %collective-permute-start = (bf16[400,128]{1,0:T(8,128)(2,1)}, bf16[400,128]{1,0:T(8,128)(2,1)S(1)}, u32[]{:S(2)}, u32[]{:S(2)}) collective-permute-start(bf16[400,128]{1,0:T(8,128)(2,1)} %get-tuple-element.11), channel_id=1, source_target_pairs={{0,64},{2,66},{4,68},{6,70},{8,72},{10,74},{12,76},{14,78},{16,80}... | collective-permute-start | bytes 307208 | tf_op jit(solution)/shard_map/ppermute | solution.py:30
  10.9 28.5 %collective-permute-start.3 = (bf16[384,128]{1,0:T(8,128)(2,1)}, bf16[384,128]{1,0:T(8,128)(2,1)S(1)}, u32[]{:S(2)}, u32[]{:S(2)}) collective-permute-start(bf16[384,128]{1,0:T(8,128)(2,1)} %get-tuple-element.12), channel_id=1, source_target_pairs={{0,66},{2,64},{4,70},{6,68},{8,74},{10,72},{12,78},{14,76},{16,82}... | collective-permute-start | bytes 294920 | tf_op jit(solution)/shard_map/ppermute | solution.py:30
  39.4 39.6 %collective-permute-start.2 = (bf16[64,64,128]{2,1,0:T(8,128)(2,1)S(1)}, bf16[64,64,128]{2,1,0:T(8,128)(2,1)S(1)}, u32[]{:S(2)}, u32[]{:S(2)}) collective-permute-start(bf16[64,64,128]{2,1,0:T(8,128)(2,1)S(1)} %collective-permute-done.1.refs_2_), channel_id=1, source_target_pairs={{0,2},{2,0},{4,6},{6,4},{8,10},{10,8},{12,14},{14,12},{16,18},{18,... | collective-permute-start | bytes 3145736 | tf_op jit(solution)/shard_map/ppermute | solution.py:30
  60.6 11.9 %collective-permute-start.6 = (bf16[1536,128]{1,0:T(8,128)(2,1)}, bf16[1536,128]{1,0:T(8,128)(2,1)S(1)}, u32[]{:S(2)}, u32[]{:S(2)}) collective-permute-start(bf16[1536,128]{1,0:T(8,128)(2,1)} %get-tuple-element.17), channel_id=1, source_target_pairs={{0,16},{2,18},{4,20},{6,22},{8,24},{10,26},{12,28},{14,30},{16,32}... | collective-permute-start | bytes 1179656 | tf_op jit(solution)/shard_map/ppermute | solution.py:30
  63.7 10.7 %collective-permute-start.8 = (bf16[1536,128]{1,0:T(8,128)(2,1)}, bf16[1536,128]{1,0:T(8,128)(2,1)}, u32[]{:S(2)}, u32[]{:S(2)}) collective-permute-start(bf16[1536,128]{1,0:T(8,128)(2,1)} %get-tuple-element.18), channel_id=1, source_target_pairs={{0,48},{2,50},{4,52},{6,54},{8,56},{10,58},{12,60},{14,62},{16,0},... | collective-permute-start | bytes 1179656 | tf_op jit(solution)/shard_map/ppermute | solution.py:30
  67.2 22.2 %collective-permute-start.5 = (bf16[1536,128]{1,0:T(8,128)(2,1)}, bf16[1536,128]{1,0:T(8,128)(2,1)S(1)}, u32[]{:S(2)}, u32[]{:S(2)}) collective-permute-start(bf16[1536,128]{1,0:T(8,128)(2,1)} %get-tuple-element.17), channel_id=1, source_target_pairs={{0,48},{2,50},{4,52},{6,54},{8,56},{10,58},{12,60},{14,62},{16,0},... | collective-permute-start | bytes 1179656 | tf_op jit(solution)/shard_map/ppermute | solution.py:30
  70.3 19.1 %collective-permute-start.4 = (bf16[1536,128]{1,0:T(8,128)(2,1)}, bf16[1536,128]{1,0:T(8,128)(2,1)S(1)}, u32[]{:S(2)}, u32[]{:S(2)}) collective-permute-start(bf16[1536,128]{1,0:T(8,128)(2,1)} %get-tuple-element.18), channel_id=1, source_target_pairs={{0,16},{2,18},{4,20},{6,22},{8,24},{10,26},{12,28},{14,30},{16,32}... | collective-permute-start | bytes 1179656 | tf_op jit(solution)/shard_map/ppermute | solution.py:30
  72.5 17.0 %collective-permute-start.7 = (bf16[1536,128]{1,0:T(8,128)(2,1)S(1)}, bf16[1536,128]{1,0:T(8,128)(2,1)S(1)}, u32[]{:S(2)}, u32[]{:S(2)}) collective-permute-start(bf16[1536,128]{1,0:T(8,128)(2,1)S(1)} %collective-permute-done.6), channel_id=1, source_target_pairs={{0,16},{2,18},{4,20},{6,22},{8,24},{10,26},{12,28},{14,30},{16,32}... | collective-permute-start | bytes 1179656 | tf_op jit(solution)/shard_map/ppermute | solution.py:30
  74.4 15.0 %collective-permute-start.9 = (bf16[1536,128]{1,0:T(8,128)(2,1)}, bf16[1536,128]{1,0:T(8,128)(2,1)S(1)}, u32[]{:S(2)}, u32[]{:S(2)}) collective-permute-start(bf16[1536,128]{1,0:T(8,128)(2,1)} %collective-permute-done.8), channel_id=1, source_target_pairs={{0,48},{2,50},{4,52},{6,54},{8,56},{10,58},{12,60},{14,62},{16,0},... | collective-permute-start | bytes 1179656 | tf_op jit(solution)/shard_map/ppermute | solution.py:30
  100.0 11.6 %collective-permute-start.10 = (bf16[64,32,128]{2,1,0:T(8,128)(2,1)S(1)}, bf16[64,32,128]{2,1,0:T(8,128)(2,1)S(1)}, u32[]{:S(2)}, u32[]{:S(2)}) collective-permute-start(bf16[64,32,128]{2,1,0:T(8,128)(2,1)S(1)} %get-tuple-element.15), channel_id=1, source_target_pairs={{0,2},{2,0},{4,6},{6,4},{8,10},{10,8},{12,14},{14,12},{16,18},{18,... | collective-permute-start | bytes 1572872 | tf_op jit(solution)/shard_map/ppermute | solution.py:30
where the time goes:
time: 113 us
  starting transfers between devices  44.2 us (39%)
  waiting for transfers between devices  24.9 us (22%)
  Pallas kernels  24.3 us (22%)
  blocking collectives  18.3 us (16%)
    ppermute x11, starting transfers between devices, moved(): return lax.ppermute(value, FLAT, pairs)  44.2 us
    ppermute x11, waiting for transfers between devices, moved(): return lax.ppermute(value, FLAT, pairs)  24.9 us
    pallas_call x2, Pallas kernels, stage(): pl.pallas_call(body, grid_spec=pltpu.PrefetchScalarGridSpec(num_scalar_pr...  20.9 us
    all_gather x1, blocking collectives, relay(): line = lax.all_gather(mine, 'y', axis=0, tiled=True)  18.3 us
  transfers between devices with their start and end apart: 11, of which 3 were waited for; matrix products, arithmetic and copies ran while one was open for 1% of the time, Pallas kernels for 11%

commit v1 on v0

--- a/solution.py
+++ b/solution.py
@@ -238,35 +238,6 @@
     )(place, *operands)
 
 
-def put_body(place_ref, part_ref, whole_ref, out_ref, sems):
-    tok, heads = part_ref.shape[:2]
-    count = sems.shape[0]
-    step = tok // count
-    copies = []
-    for n in range(count):
-        span = pl.ds(n * step, step)
-        target = out_ref.at[span, pl.ds((1 - place_ref[2]) * heads, heads)]
-        copies.append(pltpu.make_async_copy(part_ref.at[span], target, sems.at[n]))
-    for copy in copies:
-        copy.start()
-    for copy in copies:
-        copy.wait()
-
-
-def put(place, part, whole):
-    raw = pl.BlockSpec(memory_space=pl.ANY)
-    return pl.pallas_call(
-        put_body,
-        out_shape=jax.ShapeDtypeStruct(whole.shape, whole.dtype),
-        in_specs=[pl.BlockSpec(memory_space=pltpu.SMEM), raw, raw],
-        out_specs=raw,
-        scratch_shapes=[pltpu.SemaphoreType.DMA((4,))],
-        input_output_aliases={2: 0},
-        compiler_params=pltpu.CompilerParams(vmem_limit_bytes=1 << 20),
-        name="put",
-    )(place, part, whole)
-
-
 def on_device(queries, span_keys, span_values, cache_keys, cache_values, scale_exps, block_order, sizes):
     return relay(queries, span_keys, span_values, cache_keys, cache_values, scale_exps, block_order, sizes)
 
@@ -303,7 +274,7 @@
     spots = [(nx - 1, mid), (1, 0), (2, 0), (2, mid)]
     result, theirs = stage(place, order, [q_own, q_other], chunks, spots, state, tok, cache, last=True, ahead=3)
     theirs = moved(theirs, sizes, dc=1)
-    return put(place, theirs, result)[None]
+    return lax.dynamic_update_slice(result, theirs, (0, (1 - core) * theirs.shape[1], 0))[None]
 
 
 def solution(mesh):

time: 113 us -> 113 us (level)
  Pallas kernels: 24.3 us -> 23 us
    pallas_call x1 -> x0, Pallas kernels: 1.36 us -> none  [put(): pl.pallas_call(put_body, out_shape=jax.ShapeDtypeStruct(whole.shape, whol...]
where the time goes in v1:
time: 113 us; the launch traced here: 112 us
  starting transfers between devices  44.2 us (39%)
  waiting for transfers between devices  24.9 us (22%)
  Pallas kernels  23 us (20%)
  blocking collectives  18.3 us (16%)
  local copies, waits for them, and re-layouts  1.81 us (2%)
    ppermute x11, starting transfers between devices, moved(): return lax.ppermute(value, FLAT, pairs)  44.2 us
    ppermute x11, waiting for transfers between devices, moved(): return lax.ppermute(value, FLAT, pairs)  24.9 us
    pallas_call x2, Pallas kernels, stage(): pl.pallas_call(body, grid_spec=pltpu.PrefetchScalarGridSpec(num_scalar_pr...  20.9 us
    all_gather x1, blocking collectives, relay(): line = lax.all_gather(mine, 'y', axis=0, tiled=True)  18.3 us
  transfers between devices with their start and end apart: 11, of which 3 were waited for; matrix products, arithmetic and copies ran while one was open for 1% of the time, Pallas kernels for 11%

profile of v1, /device:TPU:1, one launch (start us, length us, event | category | flops | bytes accessed | tf_op | source)
XLA Modules:
  0.0 112.5 jit_solution(66708964682581108)
XLA Ops:
  0.0 4.8 %collective-permute-start.1 = (bf16[64,64,128]{2,1,0:T(8,128)(2,1)}, bf16[64,64,128]{2,1,0:T(8,128)(2,1)S(1)}, u32[]{:S(2)}, u32[]{:S(2)}) collective-permute-start(bf16[64,64,128]{2,1,0:T(8,128)(2,1)} %bitcast.32), channel_id=1, source_target_pairs={{0,64},{2,66},{4,68},{6,70},{8,72},{10,74},{12,76},{14,78},{16,80}... | collective-permute-start | bytes 3145736 | tf_op jit(solution)/shard_map/ppermute | solution.py:30
  4.8 2.1 %pack_kv.1 = (bf16[400,128]{1,0:T(8,128)(2,1)}, bf16[384,128]{1,0:T(8,128)(2,1)}) custom-call(s32[1]{0:T(128)} %bitcast.2.core_ref, s32[2,2,4]{2,1,0:T(2,128)} %bitcast.31, s32[1,64]{1,0:T(1,128)} %order_ref.1, bf16[256,128]{1,0:T(8,128)(2,1)} %bitcast.27, bf16[256,128]{1,0:T(8,128)(2,1)} %bitcast.28, bf16[128,128]{1,0:T(8,128)(2,1)} %bitcast.29, ...), custom_call_target="tpu_custom_call" | custom-call | tf_op jit(solution)/shard_map/pack_kv/pallas_call | solution.py:96
  6.9 4.0 %collective-permute-start = (bf16[400,128]{1,0:T(8,128)(2,1)}, bf16[400,128]{1,0:T(8,128)(2,1)S(1)}, u32[]{:S(2)}, u32[]{:S(2)}) collective-permute-start(bf16[400,128]{1,0:T(8,128)(2,1)} %get-tuple-element.11), channel_id=1, source_target_pairs={{0,64},{2,66},{4,68},{6,70},{8,72},{10,74},{12,76},{14,78},{16,80}... | collective-permute-start | bytes 307208 | tf_op jit(solution)/shard_map/ppermute | solution.py:30
  10.9 5.1 %collective-permute-start.3 = (bf16[384,128]{1,0:T(8,128)(2,1)}, bf16[384,128]{1,0:T(8,128)(2,1)S(1)}, u32[]{:S(2)}, u32[]{:S(2)}) collective-permute-start(bf16[384,128]{1,0:T(8,128)(2,1)} %get-tuple-element.12), channel_id=1, source_target_pairs={{0,66},{2,64},{4,70},{6,68},{8,74},{10,72},{12,78},{14,76},{16,82}... | collective-permute-start | bytes 294920 | tf_op jit(solution)/shard_map/ppermute | solution.py:30
  16.0 20.7 %collective-permute-done = bf16[400,128]{1,0:T(8,128)(2,1)S(1)} collective-permute-done((bf16[400,128]{1,0:T(8,128)(2,1)}, bf16[400,128]{1,0:T(8,128)(2,1)S(1)}, u32[]{:S(2)}, u32[]{:S(2)}) %collective-permute-start) | collective-permute-done | bytes 102432 | tf_op jit(solution)/shard_map/ppermute | solution.py:30
  36.7 2.7 %collective-permute-done.3 = bf16[384,128]{1,0:T(8,128)(2,1)S(1)} collective-permute-done((bf16[384,128]{1,0:T(8,128)(2,1)}, bf16[384,128]{1,0:T(8,128)(2,1)S(1)}, u32[]{:S(2)}, u32[]{:S(2)}) %collective-permute-start.3) | collective-permute-done | bytes 98336 | tf_op jit(solution)/shard_map/ppermute | solution.py:30
  39.4 0.0 collective-permute-done.1.refs_2_
  39.4 1.9 %collective-permute-start.2 = (bf16[64,64,128]{2,1,0:T(8,128)(2,1)S(1)}, bf16[64,64,128]{2,1,0:T(8,128)(2,1)S(1)}, u32[]{:S(2)}, u32[]{:S(2)}) collective-permute-start(bf16[64,64,128]{2,1,0:T(8,128)(2,1)S(1)} %collective-permute-done.1.refs_2_), channel_id=1, source_target_pairs={{0,2},{2,0},{4,6},{6,4},{8,10},{10,8},{12,14},{14,12},{16,18},{18,... | collective-permute-start | bytes 3145736 | tf_op jit(solution)/shard_map/ppermute | solution.py:30
  41.4 18.3 %all_gather.3 = bf16[3072,128]{1,0:T(8,128)(2,1)S(1)} all-gather(bf16[768,128]{1,0:T(8,128)(2,1)S(1)} %pad_maximum_fusion), channel_id=1, replica_groups=mesh['pipe'=8,'x'=4,'y'=4,'core'=2,'tp'=2] {'y'}, dimensions={0}, use_global_device_ids=true | all-gather | bytes 983040 | tf_op jit(solution)/shard_map/all_gather | solution.py:260
  59.6 0.9 fusion
  60.6 3.1 %collective-permute-start.6 = (bf16[1536,128]{1,0:T(8,128)(2,1)}, bf16[1536,128]{1,0:T(8,128)(2,1)S(1)}, u32[]{:S(2)}, u32[]{:S(2)}) collective-permute-start(bf16[1536,128]{1,0:T(8,128)(2,1)} %get-tuple-element.17), channel_id=1, source_target_pairs={{0,16},{2,18},{4,20},{6,22},{8,24},{10,26},{12,28},{14,30},{16,32}... | collective-permute-start | bytes 1179656 | tf_op jit(solution)/shard_map/ppermute | solution.py:30
  63.7 3.4 %collective-permute-start.8 = (bf16[1536,128]{1,0:T(8,128)(2,1)}, bf16[1536,128]{1,0:T(8,128)(2,1)}, u32[]{:S(2)}, u32[]{:S(2)}) collective-permute-start(bf16[1536,128]{1,0:T(8,128)(2,1)} %get-tuple-element.18), channel_id=1, source_target_pairs={{0,48},{2,50},{4,52},{6,54},{8,56},{10,58},{12,60},{14,62},{16,0},... | collective-permute-start | bytes 1179656 | tf_op jit(solution)/shard_map/ppermute | solution.py:30
  67.1 0.1 pad_add_fusion.refs_0_
  67.2 3.2 %collective-permute-start.5 = (bf16[1536,128]{1,0:T(8,128)(2,1)}, bf16[1536,128]{1,0:T(8,128)(2,1)S(1)}, u32[]{:S(2)}, u32[]{:S(2)}) collective-permute-start(bf16[1536,128]{1,0:T(8,128)(2,1)} %get-tuple-element.17), channel_id=1, source_target_pairs={{0,48},{2,50},{4,52},{6,54},{8,56},{10,58},{12,60},{14,62},{16,0},... | collective-permute-start | bytes 1179656 | tf_op jit(solution)/shard_map/ppermute | solution.py:30
  70.3 2.1 %collective-permute-start.4 = (bf16[1536,128]{1,0:T(8,128)(2,1)}, bf16[1536,128]{1,0:T(8,128)(2,1)S(1)}, u32[]{:S(2)}, u32[]{:S(2)}) collective-permute-start(bf16[1536,128]{1,0:T(8,128)(2,1)} %get-tuple-element.18), channel_id=1, source_target_pairs={{0,16},{2,18},{4,20},{6,22},{8,24},{10,26},{12,28},{14,30},{16,32}... | collective-permute-start | bytes 1179656 | tf_op jit(solution)/shard_map/ppermute | solution.py:30
  72.5 0.0 collective-permute-done.6
  72.5 1.9 %collective-permute-start.7 = (bf16[1536,128]{1,0:T(8,128)(2,1)S(1)}, bf16[1536,128]{1,0:T(8,128)(2,1)S(1)}, u32[]{:S(2)}, u32[]{:S(2)}) collective-permute-start(bf16[1536,128]{1,0:T(8,128)(2,1)S(1)} %collective-permute-done.6), channel_id=1, source_target_pairs={{0,16},{2,18},{4,20},{6,22},{8,24},{10,26},{12,28},{14,30},{16,32}... | collective-permute-start | bytes 1179656 | tf_op jit(solution)/shard_map/ppermute | solution.py:30
  74.4 0.0 collective-permute-done.8
  74.4 4.6 %collective-permute-start.9 = (bf16[1536,128]{1,0:T(8,128)(2,1)}, bf16[1536,128]{1,0:T(8,128)(2,1)S(1)}, u32[]{:S(2)}, u32[]{:S(2)}) collective-permute-start(bf16[1536,128]{1,0:T(8,128)(2,1)} %collective-permute-done.8), channel_id=1, source_target_pairs={{0,48},{2,50},{4,52},{6,54},{8,56},{10,58},{12,60},{14,62},{16,0},... | collective-permute-start | bytes 1179656 | tf_op jit(solution)/shard_map/ppermute | solution.py:30
  79.0 0.0 collective-permute-done.2.refs_3_
  79.0 10.4 %stage.1 = (f32[2,2048,256]{2,1,0:T(8,128)S(1)}, f32[2,2048,128]{2,1,0:T(8,128)S(1)}) custom-call(s32[5]{0:T(128)S(1)} %pad_add_fusion.refs_0_, s32[1,64]{1,0:T(1,128)S(1)} %slice_convert_fusion.refs_1_, bf16[64,64,128]{2,1,0:T(8,128)(2,1)S(1)} %collective-permute-done.1.refs_2_, bf16[64,64,128]{2,1,0:T(8,128)(2,1)S(1)} %collective-permute-done.2.refs_3_, ...), custom_call_target="tpu_custom_call" | custom-call | flops 6442450944 | bytes 12582912 | tf_op jit(solution)/shard_map/stage/pallas_call | solution.py:225
  89.4 0.0 collective-permute-done.5
  89.4 0.0 collective-permute-done.4
  89.4 0.0 collective-permute-done.7
  89.4 0.0 collective-permute-done.9
  89.4 10.5 %stage_last.1 = (bf16[64,64,128]{2,1,0:T(8,128)(2,1)}, bf16[64,32,128]{2,1,0:T(8,128)(2,1)S(1)}) custom-call(s32[5]{0:T(128)S(1)} %pad_add_fusion.refs_0_, s32[1,64]{1,0:T(1,128)S(1)} %slice_convert_fusion.refs_1_, bf16[64,64,128]{2,1,0:T(8,128)(2,1)S(1)} %collective-permute-done.1.refs_2_, bf16[64,64,128]{2,1,0:T(8,128)(2,1)S(1)} %collective-permute-done.2.refs_3_, ...), custom_call_target="tpu_custom_call" | custom-call | flops 6442450944 | bytes 12582912 | tf_op jit(solution)/shard_map/stage_last/pallas_call | solution.py:225
  100.0 10.1 %collective-permute-start.10 = (bf16[64,32,128]{2,1,0:T(8,128)(2,1)S(1)}, bf16[64,32,128]{2,1,0:T(8,128)(2,1)S(1)}, u32[]{:S(2)}, u32[]{:S(2)}) collective-permute-start(bf16[64,32,128]{2,1,0:T(8,128)(2,1)S(1)} %get-tuple-element.16), channel_id=1, source_target_pairs={{0,2},{2,0},{4,6},{6,4},{8,10},{10,8},{12,14},{14,12},{16,18},{18,... | collective-permute-start | bytes 1572872 | tf_op jit(solution)/shard_map/ppermute | solution.py:30
  110.1 1.5 %collective-permute-done.10 = bf16[64,32,128]{2,1,0:T(8,128)(2,1)S(1)} collective-permute-done((bf16[64,32,128]{2,1,0:T(8,128)(2,1)S(1)}, bf16[64,32,128]{2,1,0:T(8,128)(2,1)S(1)}, u32[]{:S(2)}, u32[]{:S(2)}) %collective-permute-start.10) | collective-permute-done | bytes 524320 | tf_op jit(solution)/shard_map/ppermute | solution.py:30
  111.6 0.9 bitcast_dynamic-update-slice_fusion
  (4 shorter events, 0.0 us)
Async XLA Ops:
  0.0 39.4 %collective-permute-start.1 = (bf16[64,64,128]{2,1,0:T(8,128)(2,1)}, bf16[64,64,128]{2,1,0:T(8,128)(2,1)S(1)}, u32[]{:S(2)}, u32[]{:S(2)}) collective-permute-start(bf16[64,64,128]{2,1,0:T(8,128)(2,1)} %bitcast.32), channel_id=1, source_target_pairs={{0,64},{2,66},{4,68},{6,70},{8,72},{10,74},{12,76},{14,78},{16,80}... | collective-permute-start | bytes 3145736 | tf_op jit(solution)/shard_map/ppermute | solution.py:30
  6.9 29.9 %collective-permute-start = (bf16[400,128]{1,0:T(8,128)(2,1)}, bf16[400,128]{1,0:T(8,128)(2,1)S(1)}, u32[]{:S(2)}, u32[]{:S(2)}) collective-permute-start(bf16[400,128]{1,0:T(8,128)(2,1)} %get-tuple-element.11), channel_id=1, source_target_pairs={{0,64},{2,66},{4,68},{6,70},{8,72},{10,74},{12,76},{14,78},{16,80}... | collective-permute-start | bytes 307208 | tf_op jit(solution)/shard_map/ppermute | solution.py:30
  10.9 28.5 %collective-permute-start.3 = (bf16[384,128]{1,0:T(8,128)(2,1)}, bf16[384,128]{1,0:T(8,128)(2,1)S(1)}, u32[]{:S(2)}, u32[]{:S(2)}) collective-permute-start(bf16[384,128]{1,0:T(8,128)(2,1)} %get-tuple-element.12), channel_id=1, source_target_pairs={{0,66},{2,64},{4,70},{6,68},{8,74},{10,72},{12,78},{14,76},{16,82}... | collective-permute-start | bytes 294920 | tf_op jit(solution)/shard_map/ppermute | solution.py:30
  39.4 39.6 %collective-permute-start.2 = (bf16[64,64,128]{2,1,0:T(8,128)(2,1)S(1)}, bf16[64,64,128]{2,1,0:T(8,128)(2,1)S(1)}, u32[]{:S(2)}, u32[]{:S(2)}) collective-permute-start(bf16[64,64,128]{2,1,0:T(8,128)(2,1)S(1)} %collective-permute-done.1.refs_2_), channel_id=1, source_target_pairs={{0,2},{2,0},{4,6},{6,4},{8,10},{10,8},{12,14},{14,12},{16,18},{18,... | collective-permute-start | bytes 3145736 | tf_op jit(solution)/shard_map/ppermute | solution.py:30
  60.6 11.9 %collective-permute-start.6 = (bf16[1536,128]{1,0:T(8,128)(2,1)}, bf16[1536,128]{1,0:T(8,128)(2,1)S(1)}, u32[]{:S(2)}, u32[]{:S(2)}) collective-permute-start(bf16[1536,128]{1,0:T(8,128)(2,1)} %get-tuple-element.17), channel_id=1, source_target_pairs={{0,16},{2,18},{4,20},{6,22},{8,24},{10,26},{12,28},{14,30},{16,32}... | collective-permute-start | bytes 1179656 | tf_op jit(solution)/shard_map/ppermute | solution.py:30
  63.7 10.7 %collective-permute-start.8 = (bf16[1536,128]{1,0:T(8,128)(2,1)}, bf16[1536,128]{1,0:T(8,128)(2,1)}, u32[]{:S(2)}, u32[]{:S(2)}) collective-permute-start(bf16[1536,128]{1,0:T(8,128)(2,1)} %get-tuple-element.18), channel_id=1, source_target_pairs={{0,48},{2,50},{4,52},{6,54},{8,56},{10,58},{12,60},{14,62},{16,0},... | collective-permute-start | bytes 1179656 | tf_op jit(solution)/shard_map/ppermute | solution.py:30
  67.2 22.2 %collective-permute-start.5 = (bf16[1536,128]{1,0:T(8,128)(2,1)}, bf16[1536,128]{1,0:T(8,128)(2,1)S(1)}, u32[]{:S(2)}, u32[]{:S(2)}) collective-permute-start(bf16[1536,128]{1,0:T(8,128)(2,1)} %get-tuple-element.17), channel_id=1, source_target_pairs={{0,48},{2,50},{4,52},{6,54},{8,56},{10,58},{12,60},{14,62},{16,0},... | collective-permute-start | bytes 1179656 | tf_op jit(solution)/shard_map/ppermute | solution.py:30
  70.3 19.1 %collective-permute-start.4 = (bf16[1536,128]{1,0:T(8,128)(2,1)}, bf16[1536,128]{1,0:T(8,128)(2,1)S(1)}, u32[]{:S(2)}, u32[]{:S(2)}) collective-permute-start(bf16[1536,128]{1,0:T(8,128)(2,1)} %get-tuple-element.18), channel_id=1, source_target_pairs={{0,16},{2,18},{4,20},{6,22},{8,24},{10,26},{12,28},{14,30},{16,32}... | collective-permute-start | bytes 1179656 | tf_op jit(solution)/shard_map/ppermute | solution.py:30
  72.5 17.0 %collective-permute-start.7 = (bf16[1536,128]{1,0:T(8,128)(2,1)S(1)}, bf16[1536,128]{1,0:T(8,128)(2,1)S(1)}, u32[]{:S(2)}, u32[]{:S(2)}) collective-permute-start(bf16[1536,128]{1,0:T(8,128)(2,1)S(1)} %collective-permute-done.6), channel_id=1, source_target_pairs={{0,16},{2,18},{4,20},{6,22},{8,24},{10,26},{12,28},{14,30},{16,32}... | collective-permute-start | bytes 1179656 | tf_op jit(solution)/shard_map/ppermute | solution.py:30
  74.4 15.0 %collective-permute-start.9 = (bf16[1536,128]{1,0:T(8,128)(2,1)}, bf16[1536,128]{1,0:T(8,128)(2,1)S(1)}, u32[]{:S(2)}, u32[]{:S(2)}) collective-permute-start(bf16[1536,128]{1,0:T(8,128)(2,1)} %collective-permute-done.8), channel_id=1, source_target_pairs={{0,48},{2,50},{4,52},{6,54},{8,56},{10,58},{12,60},{14,62},{16,0},... | collective-permute-start | bytes 1179656 | tf_op jit(solution)/shard_map/ppermute | solution.py:30
  100.0 11.6 %collective-permute-start.10 = (bf16[64,32,128]{2,1,0:T(8,128)(2,1)S(1)}, bf16[64,32,128]{2,1,0:T(8,128)(2,1)S(1)}, u32[]{:S(2)}, u32[]{:S(2)}) collective-permute-start(bf16[64,32,128]{2,1,0:T(8,128)(2,1)S(1)} %get-tuple-element.16), channel_id=1, source_target_pairs={{0,2},{2,0},{4,6},{6,4},{8,10},{10,8},{12,14},{14,12},{16,18},{18,... | collective-permute-start | bytes 1572872 | tf_op jit(solution)/shard_map/ppermute | solution.py:30
